TPU v7x, 32 devices: a whole 2x2x4 slice. The times are simulated.
32 devices in a mesh: ga: 16 (over z, y, x), band: 2 (over core).
Axes of the slice: x: 2, y: 2, z: 4, core: 2. Of those that a mesh axis runs over, the one named last changes fastest.
Arguments:
- coefficients: float32 [2048, 2, 8192], P('band', None, 'ga'), may hold values from -6 to 6
- rotation: float32 [2, 2048, 32], P(None, 'band', 'ga'), may hold values from -0.125 to 0.125
- potential: float32 [64, 4096], P(None, 'ga'), may hold values from -2 to 0.5
- index_map: int32 [8192], replicated, may hold values from 0 to 262143, as said below
- counts: int32 [16], replicated, may hold values from 384 to 512, as said below
Outputs:
- applied_panel: float32 [32, 2, 32, 1024], P(('band', 'ga'))
Inputs may be any that keep to these rules, and one draw needn't show every extreme that they name: counts[i] counts the live slots of index i of ga, which are its slots 0 to counts[i] - 1 of 512; the counts sum to 7168, and some index has exactly 512. `index_map`: live slots name distinct cells, and together exactly 7168 cells whose signed frequency vector has a squared length no larger than that of any cell not named (a ball about the anchor), every signed component of a live cell lying in -16 to 15; dead slots name arbitrary cells.
All inputs are finite; a program needn't handle non-finite values.
Results may differ from a plain program's by a relative error of at most 0.00008.
Values sent between devices are 32-bit elements; how exact they have to be, the bound alone decides.
A program may use at most 128 MiB of HBM per device.

v0:
```python
import math

import jax
import jax.numpy as jnp
from jax import lax
from jax.sharding import PartitionSpec as P


def mixing(columns):
    real_cols = columns[0].T
    imag_cols = columns[1].T
    upper_rows = jnp.stack([real_cols, -imag_cols], axis=-1)
    lower_rows = jnp.stack([imag_cols, real_cols], axis=-1)
    stacked = jnp.stack([upper_rows, lower_rows], axis=1)
    return stacked.reshape(2 * real_cols.shape[0], 2 * real_cols.shape[1])


def window_kinetic(box_edge, window):
    signed = (jnp.arange(window, dtype=jnp.int32) - window // 2).astype(jnp.float32)
    squared = signed[:, None, None] ** 2 + signed[None, :, None] ** 2 + signed[None, None, :] ** 2
    return 8.0 / (box_edge * box_edge) * squared


def dft_tables(box_edge, window):
    signed = jnp.arange(window, dtype=jnp.int32) - window // 2
    ticks_index = jnp.arange(box_edge, dtype=jnp.int32)
    inv_phase = ticks_index[:, None] * signed[None, :] % box_edge
    inv_angles = inv_phase.astype(jnp.float32) * (2.0 * math.pi / box_edge)
    inv_cos = jnp.cos(inv_angles)
    inv_sin = jnp.sin(inv_angles)
    inverse = (
        jnp.stack([jnp.stack([inv_cos, -inv_sin], 1), jnp.stack([inv_sin, inv_cos], 1)], 0)
        / box_edge
    )
    fwd_phase = signed[:, None] * ticks_index[None, :] % box_edge
    fwd_angles = fwd_phase.astype(jnp.float32) * (2.0 * math.pi / box_edge)
    fwd_cos = jnp.cos(fwd_angles)
    fwd_sin = jnp.sin(fwd_angles)
    forward = jnp.stack([jnp.stack([fwd_cos, fwd_sin], 1), jnp.stack([-fwd_sin, fwd_cos], 1)], 0)
    return (forward, inverse)


def transform(grid_field, dft_table):
    grid_field = jnp.einsum(
        "dkcn,cnyz->dkyz", dft_table, grid_field, precision=lax.Precision.HIGHEST
    )
    grid_field = jnp.einsum(
        "dkcn,cxnz->dxkz", dft_table, grid_field, precision=lax.Precision.HIGHEST
    )
    return jnp.einsum("dkcn,cxyn->dxyk", dft_table, grid_field, precision=lax.Precision.HIGHEST)


def per_device(coefficients, rotation, potential, index_map, counts):
    rot_full, pot_full = (
        lax.all_gather(rotation, "ga", axis=2, tiled=True),
        lax.all_gather(potential, "ga", axis=1, tiled=True),
    )
    band_local = coefficients.shape[0]
    slot_local = coefficients.shape[2]
    flat_coeffs = coefficients.reshape(2 * band_local, slot_local)
    box_edge = pot_full.shape[0]
    window = box_edge // 2
    half_window = window // 2
    window_cells = window * window * window
    slots_each = index_map.shape[0] // counts.shape[0]
    slot_ids = jnp.arange(slots_each, dtype=jnp.int32)
    live_mask = (slot_ids[None, :] < counts[:, None]).reshape(-1).astype(jnp.float32)
    cell_x = (index_map // (box_edge * box_edge) + half_window) % box_edge
    cell_y = (index_map // box_edge % box_edge + half_window) % box_edge
    cell_z = (index_map % box_edge + half_window) % box_edge
    inside = (cell_x < window) & (cell_y < window) & (cell_z < window)
    window_index = jnp.where(inside, (cell_x * window + cell_y) * window + cell_z, window_cells)
    kinetic = window_kinetic(box_edge, window)
    pot_grid = pot_full.reshape(box_edge, box_edge, box_edge)
    forward, inverse = dft_tables(box_edge, window)

    def apply_one(values):
        masked = values * live_mask[None, :]
        box_cells = (
            jnp.zeros((2, window_cells), jnp.float32).at[:, window_index].add(masked, mode="drop")
        )
        grid_field = box_cells.reshape(2, window, window, window)
        real_space = transform(grid_field, inverse)
        applied = transform(pot_grid[None] * real_space, forward) + kinetic[None] * grid_field
        return applied.reshape(2, window, window * window)

    panel_rows = rot_full.shape[2] // lax.axis_size("band")
    product = jnp.dot(mixing(rot_full), flat_coeffs, precision=lax.Precision.HIGHEST)
    summed = lax.psum_scatter(
        product.reshape(panel_rows * lax.axis_size("band"), 2, slot_local),
        "band",
        scatter_dimension=0,
        tiled=True,
    )
    groups = lax.axis_size("ga")
    grouped = summed.reshape(groups, panel_rows // groups, 2, slot_local)
    return lax.map(
        apply_one, lax.all_to_all(grouped, "ga", split_axis=0, concat_axis=3, tiled=True)[0]
    )


def solution(mesh):
    placed = (P("band", None, "ga"), P(None, "band", "ga"), P(None, "ga"), P(), P())
    return jax.shard_map(
        per_device,
        mesh=mesh,
        in_specs=placed,
        out_specs=P(("band", "ga"), None, None, None),
        check_vma=False,
    )
```

profile of v0, /device:TPU:0, one launch (start us, length us, event | category | flops | bytes accessed | tf_op | source)
XLA Modules:
  0.0 186.3 jit_solution(3820941070215148177)
XLA Ops:
  7.4 0.8 copy.26
  8.1 43.8 %all_gather.7 = f32[2,1024,32]{1,0,2:T(2,128)S(1)} all-gather(f32[2,1024,2]{1,0,2:T(2,128)S(1)} %copy.26), channel_id=1, replica_groups=mesh['ga'=16,'band'=2] {'ga'}, dimensions={2}, use_global_device_ids=true | all-gather | bytes 278528 | tf_op jit(solution)/shard_map/all_gather | solution.py:55
  51.9 0.2 fusion.74
  52.2 0.1 copy_bitcast_fusion
  52.3 6.0 %fusion.19 = f32[32,2,512]{2,0,1:T(8,128)} fusion(f32[1024,2,512]{2,1,0:T(2,128)} %param.5, f32[32,1,1024,2]{2,0,3,1:T(8,128)S(1)} %get-tuple-element.24, f32[32,1,1024,2]{2,0,3,1:T(8,128)S(1)} %get-tuple-element.23), kind=kOutput, calls=%fused_computation.19 | convolution fusion | flops 805437440 | bytes 4849664 | tf_op jit(solution)/shard_map/dot_general | solution.py:88
  58.3 0.0 reduce-scatter.2.cloned.1.call-update
  58.3 0.0 all-gather.2.cloned.1.call-start
  58.3 0.5 all-gather.2.cloned.1.call-update
  58.9 0.2 fusion.63
  59.1 0.2 fusion.60
  59.2 0.1 broadcast_add_fusion
  59.3 0.1 compare_select_fusion
  59.4 0.1 convert_bitcast_fusion
  59.5 1.0 add_multiply_fusion
  60.5 1.4 reduce-scatter.2.cloned.1.call-done
  61.9 1.5 copy.30
  63.4 6.8 %all-to-all-start = ((f32[16,1,2,512]{3,2,1,0:T(2,128)}), f32[16,1,2,512]{3,2,1,0:T(2,128)S(1)}, u32[]{:S(2)}, u32[]{:S(2)}) async-start(f32[16,1,2,512]{3,2,1,0:T(2,128)} %copy.30), calls=%async_computation.1 | async-start | bytes 131072 | tf_op jit(solution)/shard_map/all_to_all | solution.py:98
  70.3 7.5 %all-to-all-done = f32[16,1,2,512]{3,2,1,0:T(2,128)S(1)} async-done(((f32[16,1,2,512]{3,2,1,0:T(2,128)}), f32[16,1,2,512]{3,2,1,0:T(2,128)S(1)}, u32[]{:S(2)}, u32[]{:S(2)}) %all-to-all-start) | async-done | bytes 65568 | tf_op jit(solution)/shard_map/all_to_all | solution.py:98
  77.8 2.6 %copy.31 = f32[8192,2]{1,0:T(8,128)} copy(f32[8192,2]{0,1:T(2,128)S(1)} %multiply_bitcast_fusion) | data formatting | bytes 131072 | tf_op jit(solution)/shard_map/while/body/eval_jaxpr/mul | solution.py:78
  80.5 51.1 %scatter_custom_fusion = f32[2,32768]{0,1:T(8,128)} fusion(s32[8192]{0:T(1024)S(1)} %compare_select_fusion, f32[8192,2]{1,0:T(8,128)} %copy.31, f32[]{:T(128)} %constant.98.clone.1), kind=kCustom, calls=%fused_computation.1 | custom fusion | flops 16384 | bytes 262656 | tf_op jit(solution)/shard_map/while/body/eval_jaxpr/scatter-add | solution.py:80
  131.5 10.7 %copy.33 = f32[2,32,32,32]{1,3,0,2:T(8,128)S(1)} copy(f32[2,32,32,32]{0,3,2,1:T(8,128)} %bitcast.124) | data formatting | bytes 524288 | tf_op jit(solution)/shard_map/while/body/eval_jaxpr/reshape | solution.py:82
  142.2 10.3 %copy.37 = f32[2,32,32,32]{3,2,0,1:T(8,128)S(1)} copy(f32[2,32,32,32]{0,3,2,1:T(8,128)} %bitcast.125) | data formatting | bytes 524288 | tf_op jit(solution)/shard_map/while/body/eval_jaxpr/reshape | solution.py:82
  152.5 2.0 %convolution_bitcast_fusion.1 = f32[2,64,32,32,1]{1,3,2,0,4:T(8,128)} fusion(f32[2,32,32,32]{1,3,0,2:T(8,128)S(1)} %copy.33, f32[1,64,2,32]{1,3,2,0:T(8,128)S(1)} %get-tuple-element.38, f32[1,64,2,32]{1,3,2,0:T(8,128)S(1)} %get-tuple-element.36), kind=kOutput, calls=%fused_computation.17 | convolution fusion | flops 100679680 | bytes 819200 | tf_op jit(solution)/shard_map/while/body/eval_jaxpr/dkcn,cnyz->dkyz/dot_general | solution.py:44
  154.5 3.0 %copy.42 = f32[2,64,32,32,1]{2,3,0,4,1:T(8,128)S(1)} copy(f32[2,64,32,32,1]{1,3,2,0,4:T(8,128)} %convolution_bitcast_fusion.1) | data formatting | bytes 1048576 | tf_op jit(solution)/shard_map/while/body/eval_jaxpr/dkcn,cnyz->dkyz/dot_general | solution.py:44
  157.5 3.2 %fusion.29 = f32[64,32,2,64,1]{3,1,4,2,0:T(8,128)} fusion(f32[2,64,32,32,1]{2,3,0,4,1:T(8,128)S(1)} %copy.42, f32[1,64,2,32]{1,3,2,0:T(8,128)S(1)} %get-tuple-element.38, f32[1,64,2,32]{1,3,2,0:T(8,128)S(1)} %get-tuple-element.36), kind=kOutput, calls=%fused_computation.36 | convolution fusion | flops 201342976 | bytes 1605632 | tf_op jit(solution)/shard_map/while/body/eval_jaxpr/dkcn,cxnz->dxkz/dot_general | solution.py:47
  160.7 3.2 %mul.208 = f32[64,64,64]{2,1,0:T(8,128)} reshape(f32[64,4096]{1,0:T(8,128)} %all-gather.2.cloned.1.call-done) | data formatting | bytes 2097152 | tf_op jit(solution)/shard_map/while/body/eval_jaxpr/mul | solution.py:84
  163.9 5.2 %fusion.4 = f32[2,64,64,64]{3,2,0,1:T(8,128)S(1)} fusion(f32[64,32,2,64,1]{3,1,4,2,0:T(8,128)S(1)} %copy-done, f32[64,64,64]{2,1,0:T(8,128)} %mul.208, f32[1,64,2,32]{1,3,2,0:T(8,128)S(1)} %get-tuple-element.38, f32[1,64,2,32]{1,3,2,0:T(8,128)S(1)} %get-tuple-element.36), kind=kOutput, calls=%fused_computation.6 | convolution fusion | flops 403193856 | bytes 4227072 | tf_op jit(solution)/shard_map/while/body/eval_jaxpr/dkcn,cxyn->dxyk/dot_general | solution.py:50
  169.1 4.8 %fusion.12 = f32[2,32,64,64,1]{3,1,2,0,4:T(8,128)S(1)} fusion(f32[2,64,64,64]{3,2,0,1:T(8,128)S(1)} %fusion.4, f32[1,32,2,64]{3,1,2,0:T(8,128)S(1)} %get-tuple-element.26, f32[1,32,2,64]{3,1,2,0:T(8,128)S(1)} %get-tuple-element.25), kind=kOutput, calls=%fused_computation.14 | convolution fusion | flops 402661376 | bytes 3178496 | tf_op jit(solution)/shard_map/while/body/eval_jaxpr/dkcn,cnyz->dkyz/dot_general | solution.py:44
  173.9 2.5 %fusion.15 = f32[2,32,32,64,1]{3,2,0,4,1:T(8,128)S(1)} fusion(f32[2,32,64,64,1]{3,1,2,0,4:T(8,128)S(1)} %fusion.12, f32[1,32,2,64]{3,1,2,0:T(8,128)S(1)} %get-tuple-element.26, f32[1,32,2,64]{3,1,2,0:T(8,128)S(1)} %get-tuple-element.25), kind=kOutput, calls=%fused_computation.15 | convolution fusion | flops 201334784 | bytes 1605632 | tf_op jit(solution)/shard_map/while/body/eval_jaxpr/dkcn,cxnz->dxkz/dot_general | solution.py:47
  176.4 1.0 fusion.18
  177.5 0.6 broadcast_in_dim.15
  178.0 0.8 copy.38
  (18 shorter events, 0.2 us)
Async XLA Ops:
  7.4 51.9 %copy-start.2 = (s32[8192]{0:T(1024)S(1)}, s32[8192]{0:T(1024)}, u32[]{:S(2)}) copy-start(s32[8192]{0:T(1024)} %param.8) | copy-start | bytes 98308
  7.4 52.0 %copy-start.3 = (s32[16]{0:T(128)S(1)}, s32[16]{0:T(128)}, u32[]{:S(2)}) copy-start(s32[16]{0:T(128)} %param.9) | copy-start | bytes 196
  7.4 54.5 %reduce-scatter.2.cloned.1.call-start = ((), (), s32[]{:S(2)}) async-start(), calls=%async_computation.3 | async-start | bytes 196608 | tf_op jit(solution)/shard_map/reduce_scatter | solution.py:89
  58.3 102.4 %all-gather.2.cloned.1.call-start = ((), (), s32[]{:S(2)}) async-start(), calls=%async_computation.2 | async-start | bytes 1114112 | tf_op jit(solution)/shard_map/all_gather | solution.py:56
  63.4 14.4 %all-to-all-start = ((f32[16,1,2,512]{3,2,1,0:T(2,128)}), f32[16,1,2,512]{3,2,1,0:T(2,128)S(1)}, u32[]{:S(2)}, u32[]{:S(2)}) async-start(f32[16,1,2,512]{3,2,1,0:T(2,128)} %copy.30), calls=%async_computation.1 | async-start | bytes 131072 | tf_op jit(solution)/shard_map/all_to_all | solution.py:98
  160.7 3.2 %copy-start = (f32[64,32,2,64,1]{3,1,4,2,0:T(8,128)S(1)}, f32[64,32,2,64,1]{3,1,4,2,0:T(8,128)}, u32[]{:S(2)}) copy-start(f32[64,32,2,64,1]{3,1,4,2,0:T(8,128)} %fusion.29) | copy-start | bytes 3145732
  169.1 7.3 %copy-start.1 = (f32[32,32,32]{2,1,0:T(8,128)S(1)}, f32[32,32,32]{2,1,0:T(8,128)}, u32[]{:S(2)}) copy-start(f32[32,32,32]{2,1,0:T(8,128)} %add_multiply_fusion) | copy-start | bytes 393220
Sparse Core Ops, SparseCore 0:
  58.4 3.4 reduce-scatter.1
Sparse Core Ops, SparseCore 1:
  61.5 48.9 all-gather.1
where the time goes:
time: 187 us; the launch traced here: 186 us
  other arithmetic  52.8 us (28%)
  blocking collectives  43.8 us (23%)
  local copies, waits for them, and re-layouts  33.7 us (18%)
  matrix products  24.7 us (13%)
  between operations  15 us (8%)
  waiting for transfers between devices  9.42 us (5%)
  starting transfers between devices  6.84 us (4%)
    scatter-add x1, other arithmetic, apply_one(): jnp.zeros((2, window_cells), jnp.float32).at[:, window_index]  51.1 us
    all_gather x1, blocking collectives, per_device(): lax.all_gather(rotation, 'ga', axis=2, tiled=True)  43.8 us
    reshape x2, local copies, waits for them, and re-layouts, apply_one(): grid_field = box_cells.reshape(2, window, window, window)  21 us
    all_to_all x1, waiting for transfers between devices, per_device(): lax.all_to_all(grouped, 'ga', split_axis=0, concat_axis=3, tiled=True)[0]  7.52 us
    all_to_all x1, starting transfers between devices, per_device(): lax.all_to_all(grouped, 'ga', split_axis=0, concat_axis=3, tiled=True)[0]  6.79 us
    dot_general x2, matrix products, transform(): jnp.einsum('dkcn,cnyz->dkyz', dft_table, grid_field, precision=lax.Precis...  6.79 us
    dot_general x2, matrix products, transform(): jnp.einsum('dkcn,cxyn->dxyk', dft_table, grid_field, precision=lax.Precis...  6.18 us
    dot_general x1, matrix products, per_device(): jnp.dot(mixing(rot_full), flat_coeffs, precision=lax.Precision.HIGHEST)  5.99 us
  transfers between devices with their start and end apart: 3, of which 2 were waited for; matrix products, arithmetic and copies ran while one was open for 46% of the time, Pallas kernels for 0%

commit v1 on v0

v1 whole, which is shorter than its diff:
```python
import functools
import math

import jax
import jax.numpy as jnp
import numpy as np
from jax import lax
from jax.experimental import pallas as pl
from jax.experimental.pallas import tpu as pltpu
from jax.sharding import PartitionSpec as P

F32 = jnp.float32
BF16 = jnp.bfloat16


def mixing(columns):
    real_cols = columns[0].T
    imag_cols = columns[1].T
    upper_rows = jnp.stack([real_cols, -imag_cols], axis=-1)
    lower_rows = jnp.stack([imag_cols, real_cols], axis=-1)
    stacked = jnp.stack([upper_rows, lower_rows], axis=1)
    return stacked.reshape(2 * real_cols.shape[0], 2 * real_cols.shape[1])


def split_parts(values):
    high = values.astype(BF16)
    return high, (values - high.astype(F32)).astype(BF16)


def two_parts(table):
    high = table.astype(BF16)
    low = (table - high.astype(np.float32)).astype(BF16)
    return np.stack([high, low])


def tables(box, window, radix):
    half = window // 2
    coarse = window // radix
    k_all = np.arange(box)
    k_coarse = np.arange(box // radix)
    n_signed = np.arange(window) - half
    low = np.arange(radix)
    y_phase = (radix * np.arange(coarse) - half)[:, None] * low[None, :]
    z_phase = n_signed[:, None] * k_all[None, :]
    right = y_phase[:, None, :, None] + z_phase[None, :, None, :]
    right = right.reshape(coarse * window, radix * box) % box
    x_phase = k_all[:, None] * n_signed[None, :]
    l_phase = radix * k_coarse[:, None] * low[None, :]
    left = l_phase[:, None, :, None] + x_phase[None, :, None, :]
    left = left.reshape(k_coarse.size * box, radix * window) % box
    twist = np.repeat(low[:, None] * low[None, :], box, axis=1) % box

    def pair(phase, scale=1.0):
        angle = phase * (2.0 * math.pi / box)
        return (np.stack([np.cos(angle), np.sin(angle)]) * scale).astype(np.float32)

    right_tab = two_parts(pair(right))
    left_pair = pair(left, 1.0 / box**3)
    left_tab = two_parts(left_pair)
    back_tab = two_parts((left_pair * np.float32(box**3)).transpose(0, 2, 1).copy())
    return right_tab, left_tab, back_tab, pair(twist)


def dot3(lhs, rhs, dims=((1,), (0,))):
    def one(a, b):
        return lax.dot_general(a, b, (dims, ((), ())), preferred_element_type=F32)

    return one(lhs[0], rhs[0]) + (one(lhs[0], rhs[1]) + one(lhs[1], rhs[0]))


def block(cos, sin):
    upper = jnp.concatenate([cos, sin], axis=1)
    lower = jnp.concatenate([-sin, cos], axis=1)
    return jnp.concatenate([upper, lower], axis=0)


def apply_kernel(
    box, window, radix, chunk, val_ref, row_ref, col_ref, pot_ref, right_ref, left_ref, back_ref, twist_ref, out_ref, acc
):
    coarse = window // radix
    rows = radix * window
    cols = coarse * window
    wide = radix * box
    slots = val_ref.shape[1]
    acc[...] = jnp.zeros_like(acc)

    def scatter(step, carry):
        at = pl.ds(pl.multiple_of(step * chunk, chunk), chunk)
        row_id = row_ref[:, at]
        col_id = col_ref[:, at]
        picks = lax.broadcasted_iota(jnp.int32, (rows, chunk), 0) == row_id
        onehot = jnp.where(picks, 1.0, 0.0).astype(BF16)
        hits = lax.broadcasted_iota(jnp.int32, (cols, chunk), 0) == col_id
        high, low = split_parts(val_ref[:, at])
        high, low = high.astype(F32), low.astype(F32)
        placed = [
            jnp.where(hits, part[c : c + 1, :], 0.0).astype(BF16)
            for part in (high, low)
            for c in range(2)
        ]
        acc[...] += lax.dot_general(
            onehot,
            jnp.concatenate(placed, axis=0),
            (((1,), (1,)), ((), ())),
            preferred_element_type=F32,
        )
        return carry

    lax.fori_loop(0, slots // chunk, scatter, 0)
    grid_field = acc[:, : 2 * cols] + acc[:, 2 * cols :]

    right = [block(right_ref[i, 0], right_ref[i, 1]) for i in range(2)]
    field = dot3(split_parts(grid_field), right)
    cos = twist_ref[0][:, None, :]
    sin = twist_ref[1][:, None, :]
    real = field[:, :wide].reshape(radix, window, wide)
    imag = field[:, wide:].reshape(radix, window, wide)
    turned = jnp.concatenate(
        [
            (real * cos - imag * sin).reshape(rows, wide),
            (real * sin + imag * cos).reshape(rows, wide),
        ],
        axis=0,
    )
    left = [block(left_ref[i, 0], -left_ref[i, 1]) for i in range(2)]
    space = dot3(left, split_parts(turned))
    pot = jnp.concatenate(
        [pot_ref[:, k * wide : (k + 1) * wide] for k in range(box // radix)], axis=0
    )
    space = space * jnp.concatenate([pot, pot], axis=0)
    back = [block(back_ref[i, 0], back_ref[i, 1]) for i in range(2)]
    field = dot3(back, split_parts(space))
    real = field[:rows].reshape(radix, window, wide)
    imag = field[rows:].reshape(radix, window, wide)
    turned = jnp.concatenate(
        [
            (real * cos + imag * sin).reshape(rows, wide),
            (imag * cos - real * sin).reshape(rows, wide),
        ],
        axis=1,
    )
    applied = dot3(split_parts(turned), right, ((1,), (1,)))

    half = window // 2
    row_at = lax.broadcasted_iota(jnp.int32, (rows, cols), 0)
    col_at = lax.broadcasted_iota(jnp.int32, (rows, cols), 1)
    n_x = (row_at % window - half).astype(F32)
    n_y = (col_at // window * radix + row_at // window - half).astype(F32)
    n_z = (col_at % window - half).astype(F32)
    kinetic = (8.0 / (box * box)) * (n_x * n_x + n_y * n_y + n_z * n_z)
    applied = applied + jnp.concatenate([kinetic, kinetic], axis=1) * grid_field
    for c in range(2):
        pieces = [
            applied[lo * window : (lo + 1) * window, c * cols + hi * window : c * cols + (hi + 1) * window]
            for hi in range(coarse)
            for lo in range(radix)
        ]
        out_ref[c] = jnp.concatenate(pieces, axis=1)


def apply_band(values, row_id, col_id, pot_full, window, radix, consts):
    box = pot_full.shape[0]
    slots = values.shape[1]
    chunk = math.gcd(slots, 1024)
    vmem = pl.BlockSpec(memory_space=pltpu.VMEM)
    return pl.pallas_call(
        functools.partial(apply_kernel, box, window, radix, chunk),
        out_shape=jax.ShapeDtypeStruct((2, window, window * window), F32),
        in_specs=[vmem] * 8,
        out_specs=vmem,
        scratch_shapes=[pltpu.VMEM((radix * window, 4 * (window // radix) * window), F32)],
        compiler_params=pltpu.CompilerParams(vmem_limit_bytes=60 * 1024 * 1024),
    )(values, row_id, col_id, pot_full, *consts)


def per_device(coefficients, rotation, potential, index_map, counts):
    mixer = lax.all_gather(mixing(rotation), "ga", axis=0, tiled=True)
    pot_full = lax.all_gather(potential, "ga", axis=1, tiled=True)
    band_local = coefficients.shape[0]
    slot_local = coefficients.shape[2]
    flat_coeffs = coefficients.reshape(2 * band_local, slot_local)
    box = pot_full.shape[0]
    window = box // 2
    half = window // 2
    radix = math.isqrt(box)
    assert radix * radix == box
    slots_each = index_map.shape[0] // counts.shape[0]
    slot_ids = jnp.arange(slots_each, dtype=jnp.int32)
    live = (slot_ids[None, :] < counts[:, None]).reshape(-1)
    cell_x = (index_map // (box * box) + half) % box
    cell_y = (index_map // box % box + half) % box
    cell_z = (index_map % box + half) % box
    inside = (cell_x < window) & (cell_y < window) & (cell_z < window)
    row_id = jnp.where(live & inside, cell_y % radix * window + cell_x, -1)[None]
    col_id = (cell_y // radix * window + cell_z)[None]
    consts = [jnp.asarray(t) for t in tables(box, window, radix)]

    product = jnp.dot(mixer, flat_coeffs, precision=lax.Precision.HIGH)
    panel_rows = mixer.shape[0] // 2
    summed = lax.psum_scatter(
        product.reshape(panel_rows, 2, slot_local), "band", scatter_dimension=0, tiled=True
    )
    groups = lax.axis_size("ga")
    grouped = summed.reshape(groups, summed.shape[0] // groups, 2, slot_local)
    values = lax.all_to_all(grouped, "ga", split_axis=0, concat_axis=3, tiled=True)[0]
    return jnp.stack(
        [
            apply_band(values[i], row_id, col_id, pot_full, window, radix, consts)
            for i in range(values.shape[0])
        ]
    )


def solution(mesh):
    placed = (P("band", None, "ga"), P(None, "band", "ga"), P(None, "ga"), P(), P())
    return jax.shard_map(
        per_device,
        mesh=mesh,
        in_specs=placed,
        out_specs=P(("band", "ga"), None, None, None),
        check_vma=False,
    )
```

time: 187 us -> 139 us (0.74)
  other arithmetic: 52.8 us -> 1.56 us
  waiting for transfers between devices: 9.42 us -> 42.9 us
  local copies, waits for them, and re-layouts: 33.7 us -> 10.6 us
  matrix products: 24.7 us -> 4.4 us
  Pallas kernels: 0 us -> 12.3 us
    scatter-add x1 -> x0, other arithmetic: 51.1 us -> none  [apply_one(): jnp.zeros((2, window_cells), jnp.float32).at[:, window_index]]
    all_gather x1, waiting for transfers between devices: 0.01 us -> 32.7 us  [per_device(): pot_full = lax.all_gather(potential, 'ga', axis=1, tiled=True)]
    dot_general x7 -> x1, matrix products: 24.7 us -> 4.4 us  [per_device(): product = jnp.dot(mixer, flat_coeffs, precision=lax.Precision.HIGH)]
    reshape x3 -> x2, local copies, waits for them, and re-layouts: 22.5 us -> 7.6 us  [the longest x1 6.08 us: per_device(): flat_coeffs = coefficients.reshape(2 * band_local, slot_local)]
    pallas_call x0 -> x1, Pallas kernels: none -> 12.3 us  [apply_band(): pl.pallas_call(functools.partial(apply_kernel, box, window, radix, chunk)...]
    mul x2 -> x0, local copies, waits for them, and re-layouts: 5.86 us -> none  [the longest x1 3.23 us: apply_one(): pot_grid[None] * real_space]
    dot_general x1, local copies, waits for them, and re-layouts: 3 us -> 0.41 us  [per_device(): product = jnp.dot(mixer, flat_coeffs, precision=lax.Precision.HIGH)]
  transfers between devices with their start and end apart: 3 -> 3, of which waited for: 2 -> 3; matrix products, arithmetic and copies ran while one was open for 46% -> 2% of each run, Pallas kernels for 0% -> 0%
where the time goes in v1:
time: 139 us
  blocking collectives  45.3 us (33%)
  waiting for transfers between devices  42.9 us (31%)
  between operations  14.9 us (11%)
  Pallas kernels  12.3 us (9%)
  local copies, waits for them, and re-layouts  10.6 us (8%)
  starting transfers between devices  6.79 us (5%)
  matrix products  4.4 us (3%)
  other arithmetic  1.56 us (1%)
    all_gather x1, blocking collectives, per_device(): mixer = lax.all_gather(mixing(rotation), 'ga', axis=0, tiled=True)  45.3 us
    all_gather x1, waiting for transfers between devices, per_device(): pot_full = lax.all_gather(potential, 'ga', axis=1, tiled=True)  32.7 us
    pallas_call x1, Pallas kernels, apply_band(): pl.pallas_call(functools.partial(apply_kernel, box, window, radix, chunk)...  12.3 us
    all_to_all x1, waiting for transfers between devices, per_device(): lax.all_to_all(grouped, 'ga', split_axis=0, concat_axis=3, tiled=True)[0]  6.77 us
    all_to_all x1, starting transfers between devices, per_device(): lax.all_to_all(grouped, 'ga', split_axis=0, concat_axis=3, tiled=True)[0]  6.75 us
    reshape x1, local copies, waits for them, and re-layouts, per_device(): flat_coeffs = coefficients.reshape(2 * band_local, slot_local)  6.08 us
    dot_general x1, matrix products, per_device(): product = jnp.dot(mixer, flat_coeffs, precision=lax.Precision.HIGH)  4.4 us
    reduce_scatter x1, waiting for transfers between devices, per_device(): lax.psum_scatter(product.reshape(panel_rows, 2, slot_local), 'band', scat...  2.92 us
  transfers between devices with their start and end apart: 3, of which 3 were waited for; matrix products, arithmetic and copies ran while one was open for 2% of the time, Pallas kernels for 0%

profile of v1, /device:TPU:0, one launch (start us, length us, event | category | flops | bytes accessed | tf_op | source)
XLA Modules:
  0.0 138.8 jit_solution(2906642112866929435)
XLA Ops:
  7.4 0.0 reduce-scatter.2.cloned.1.call-start
  7.4 0.7 slice_bitcast_fusion.1
  8.1 0.7 fusion.20
  8.8 0.6 copy.12
  9.5 1.2 reshape.20
  10.7 45.3 %all-gather = f32[16,4,2048]{2,1,0:T(4,128)S(1)} all-gather(f32[1,4,2048]{2,1,0:T(4,128)S(1)} %reshape.20), channel_id=1, replica_groups=mesh['ga'=16,'band'=2] {'ga'}, dimensions={0}, use_global_device_ids=true | all-gather | bytes 557056 | tf_op jit(solution)/shard_map/all_gather | solution.py:177
  56.0 0.4 dot_general.5
  56.4 6.1 %reshape.24 = f32[2048,512,1]{1,0,2:T(8,128)} reshape(f32[1024,2,512]{2,1,0:T(2,128)} %param.9) | data formatting | bytes 8388608 | tf_op jit(solution)/shard_map/reshape | solution.py:181
  62.5 0.0 copy-start.2
  62.5 0.0 copy-start.1
  62.5 4.4 %fusion = f32[32,2,512]{2,0,1:T(8,128)} fusion(f32[2048,512,1]{1,0,2:T(8,128)} %reshape.24, f32[32,2,2048]{2,1,0:T(2,128)S(1)} %dot_general.5), kind=kOutput, calls=%fused_computation | convolution fusion | flops 402653184 | bytes 4849664 | tf_op jit(solution)/shard_map/dot_general | solution.py:198
  66.9 0.0 reduce-scatter.2.cloned.1.call-update
  66.9 0.0 all-gather.3.cloned.1.call-start
  67.0 0.5 all-gather.3.cloned.1.call-update
  67.5 0.0 copy-done.2
  67.5 0.1 fusion.15
  67.6 2.9 %reduce-scatter.2.cloned.1.call-done = f32[16,2,512]{2,0,1:T(8,128)} async-done(((f32[32,2,512]{2,0,1:T(8,128)}), f32[16,2,512]{2,0,1:T(8,128)}) %reduce-scatter.2.cloned.1.call-update) | async-done | bytes 65552 | tf_op jit(solution)/shard_map/reduce_scatter | solution.py:200
  70.6 1.5 %copy.14 = f32[16,1,2,512]{3,2,1,0:T(2,128)} copy(f32[16,1,2,512]{3,0,2,1:T(8,128)} %bitcast.39) | data formatting | bytes 131072 | tf_op jit(solution)/shard_map/reshape | solution.py:204
  72.1 6.7 %all-to-all-start = ((f32[16,1,2,512]{3,2,1,0:T(2,128)}), f32[16,1,2,512]{3,2,1,0:T(2,128)S(1)}, u32[]{:S(2)}, u32[]{:S(2)}) async-start(f32[16,1,2,512]{3,2,1,0:T(2,128)} %copy.14), calls=%async_computation.1 | async-start | bytes 131072 | tf_op jit(solution)/shard_map/all_to_all | solution.py:205
  78.8 0.0 copy-done.1
  78.8 0.8 fusion.14
  79.6 6.8 %all-to-all-done = f32[16,1,2,512]{3,2,1,0:T(2,128)S(1)} async-done(((f32[16,1,2,512]{3,2,1,0:T(2,128)}), f32[16,1,2,512]{3,2,1,0:T(2,128)S(1)}, u32[]{:S(2)}, u32[]{:S(2)}) %all-to-all-start) | async-done | bytes 65568 | tf_op jit(solution)/shard_map/all_to_all | solution.py:205
  86.4 0.0 copy-start
  86.4 32.7 %all-gather.3.cloned.1.call-done.pot_ref = f32[64,4096]{1,0:T(8,128)} async-done(((f32[64,256]{1,0:T(8,128)}), f32[64,4096]{1,0:T(8,128)}) %all-gather.3.cloned.1.call-update) | async-done | bytes 1048592 | tf_op jit(solution)/shard_map/all_gather | solution.py:178
  119.1 0.0 copy-done
  119.1 12.3 %shard_map.91 = f32[2,32,1024]{2,1,0:T(8,128)} custom-call(f32[2,8192]{1,0:T(2,128)} %bitcast.36, s32[1,8192]{1,0:T(1,128)} %bitcast.38, s32[1,8192]{1,0:T(1,128)} %bitcast.37, f32[64,4096]{1,0:T(8,128)} %all-gather.3.cloned.1.call-done.pot_ref, bf16[2,2,128,512]{3,2,1,0:T(8,128)(2,1)} %constant.92.clone.right_ref, ...), custom_call_target="tpu_custom_call" | custom-call | tf_op jit(solution)/shard_map/pallas_call | solution.py:166
  (3 shorter events, 0.0 us)
Async XLA Ops:
  7.4 63.2 %reduce-scatter.2.cloned.1.call-start = ((), (), s32[]{:S(2)}) async-start(), calls=%async_computation.2 | async-start | bytes 196608 | tf_op jit(solution)/shard_map/reduce_scatter | solution.py:200
  62.5 5.0 %copy-start.2 = (s32[16]{0:T(128)S(1)}, s32[16]{0:T(128)}, u32[]{:S(2)}) copy-start(s32[16]{0:T(128)} %param.13) | copy-start | bytes 196
  62.5 16.3 %copy-start.1 = (s32[8192]{0:T(1024)S(1)}, s32[8192]{0:T(1024)}, u32[]{:S(2)}) copy-start(s32[8192]{0:T(1024)} %param.12) | copy-start | bytes 98308
  66.9 52.1 %all-gather.3.cloned.1.call-start = ((), (), s32[]{:S(2)}) async-start(), calls=%async_computation.3 | async-start | bytes 1114112 | tf_op jit(solution)/shard_map/all_gather | solution.py:178
  72.1 14.3 %all-to-all-start = ((f32[16,1,2,512]{3,2,1,0:T(2,128)}), f32[16,1,2,512]{3,2,1,0:T(2,128)S(1)}, u32[]{:S(2)}, u32[]{:S(2)}) async-start(f32[16,1,2,512]{3,2,1,0:T(2,128)} %copy.14), calls=%async_computation.1 | async-start | bytes 131072 | tf_op jit(solution)/shard_map/all_to_all | solution.py:205
  86.4 32.7 %copy-start = (f32[16,1,2,512]{3,2,1,0:T(2,128)}, f32[16,1,2,512]{3,2,1,0:T(2,128)S(1)}, u32[]{:S(2)}) copy-start(f32[16,1,2,512]{3,2,1,0:T(2,128)S(1)} %all-to-all-done) | copy-start | bytes 196612
Sparse Core Ops, SparseCore 0:
  67.1 3.4 reduce-scatter.1
Sparse Core Ops, SparseCore 1:
  70.2 48.8 all-gather.2

commit v2 on v1

--- a/solution.py
+++ b/solution.py
@@ -11,15 +11,6 @@
 
 F32 = jnp.float32
 BF16 = jnp.bfloat16
-
-
-def mixing(columns):
-    real_cols = columns[0].T
-    imag_cols = columns[1].T
-    upper_rows = jnp.stack([real_cols, -imag_cols], axis=-1)
-    lower_rows = jnp.stack([imag_cols, real_cols], axis=-1)
-    stacked = jnp.stack([upper_rows, lower_rows], axis=1)
-    return stacked.reshape(2 * real_cols.shape[0], 2 * real_cols.shape[1])
 
 
 def split_parts(values):
@@ -74,14 +65,153 @@
     return jnp.concatenate([upper, lower], axis=0)
 
 
+def exchange_kernel(
+    bands, groups, coef_hbm, rot_ref, pot_hbm, val_ref, pot_out, coef, rots, prod, land,
+    coef_sem, rot_send, rot_recv, pot_send, pot_recv, val_send, val_recv, self_sem
+):
+    band = lax.axis_index("band")
+    me = lax.axis_index("ga")
+    total = bands * groups
+    flat = band * groups + me
+    cols = rot_ref.shape[1] // 2
+    own = land.shape[1]
+
+    loads = [
+        pltpu.make_async_copy(coef_hbm.at[:, c, :], coef.at[c], coef_sem.at[c]) for c in range(2)
+    ]
+    for load in loads:
+        load.start()
+    rot_self = pltpu.make_async_copy(rot_ref.at[0], rots.at[me], self_sem.at[0])
+    rot_self.start()
+    pot_self = pltpu.make_async_copy(pot_hbm, pot_out.at[me], self_sem.at[1])
+    pot_self.start()
+
+    barrier = pltpu.get_barrier_semaphore()
+
+    def greet(step, carry):
+        to = lax.rem(flat + step, total)
+        pl.semaphore_signal(
+            barrier, inc=1, device_id={"band": to // groups, "ga": lax.rem(to, groups)},
+            device_id_type=pl.DeviceIdType.MESH,
+        )
+        return carry
+
+    lax.fori_loop(1, total, greet, 0)
+    pl.semaphore_wait(barrier, total - 1)
+
+    def rot_copy(to, slot):
+        return pltpu.make_async_remote_copy(
+            src_ref=rot_ref.at[0], dst_ref=rots.at[slot],
+            send_sem=rot_send.at[to], recv_sem=rot_recv.at[slot],
+            device_id={"band": band, "ga": to}, device_id_type=pl.DeviceIdType.MESH,
+        )
+
+    def pot_copy(to, slot):
+        return pltpu.make_async_remote_copy(
+            src_ref=pot_hbm, dst_ref=pot_out.at[slot],
+            send_sem=pot_send.at[to], recv_sem=pot_recv.at[slot],
+            device_id={"band": band, "ga": to}, device_id_type=pl.DeviceIdType.MESH,
+        )
+
+    def val_copy(to, slot):
+        return pltpu.make_async_remote_copy(
+            src_ref=prod.at[pl.ds(to * own, own)], dst_ref=land.at[slot],
+            send_sem=val_send.at[to], recv_sem=val_recv.at[slot],
+            device_id={"band": to // groups, "ga": lax.rem(to, groups)},
+            device_id_type=pl.DeviceIdType.MESH,
+        )
+
+    def each(count, mine, act):
+        def body(step, carry):
+            act(lax.rem(mine + step, count))
+            return carry
+
+        lax.fori_loop(1, count, body, 0)
+
+    each(groups, me, lambda to: rot_copy(to, me).start())
+    each(groups, me, lambda to: pot_copy(to, me).start())
+    for load in loads:
+        load.wait()
+    rot_self.wait()
+    each(groups, me, lambda src: rot_copy(src, src).wait_recv())
+
+    panel = groups * cols
+    depth = coef.shape[1]
+    real = rots[:, :cols, :].reshape(panel, depth)
+    imag = rots[:, cols:, :].reshape(panel, depth)
+    high, low = split_parts(jnp.concatenate([real, imag], axis=0))
+    both = jnp.concatenate([high, low], axis=0)
+    terms = []
+    for c in range(2):
+        c_high, c_low = split_parts(coef[c])
+        first = jnp.dot(both, c_high, preferred_element_type=F32)
+        second = jnp.dot(high, c_low, preferred_element_type=F32)
+        terms.append(first[: 2 * panel] + (first[2 * panel :] + second))
+    prod[:, 0, :] = terms[0][:panel] - terms[1][panel:]
+    prod[:, 1, :] = terms[0][panel:] + terms[1][:panel]
+
+    val_self = pltpu.make_async_copy(prod.at[pl.ds(flat * own, own)], land.at[flat], self_sem.at[2])
+    val_self.start()
+    each(total, flat, lambda to: val_copy(to, flat).start())
+    val_self.wait()
+    each(total, flat, lambda src: val_copy(src, src).wait_recv())
+    summed = land[0:groups]
+    for b in range(1, bands):
+        summed = summed + land[b * groups : (b + 1) * groups]
+    val_ref[...] = summed
+    each(total, flat, lambda to: val_copy(to, flat).wait_send())
+    each(groups, me, lambda to: rot_copy(to, me).wait_send())
+    pot_self.wait()
+    each(groups, me, lambda src: pot_copy(src, src).wait_recv())
+    each(groups, me, lambda to: pot_copy(to, me).wait_send())
+
+
+def exchange(coefficients, rotation, potential):
+    bands, groups = lax.axis_size("band"), lax.axis_size("ga")
+    depth, _, slots = coefficients.shape
+    cols = rotation.shape[2]
+    panel = cols * groups
+    own = panel // (bands * groups)
+    rot = rotation.transpose(0, 2, 1).reshape(1, 2 * cols, depth)
+    hbm = pl.BlockSpec(memory_space=pl.ANY)
+    vmem = pl.BlockSpec(memory_space=pltpu.VMEM)
+    dma = pltpu.SemaphoreType.DMA
+    return pl.pallas_call(
+        functools.partial(exchange_kernel, bands, groups),
+        out_shape=(
+            jax.ShapeDtypeStruct((groups, own, 2, slots), F32),
+            jax.ShapeDtypeStruct((groups,) + potential.shape, F32),
+        ),
+        in_specs=[hbm, vmem, hbm],
+        out_specs=(vmem, hbm),
+        scratch_shapes=[
+            pltpu.VMEM((2, depth, slots), F32),
+            pltpu.VMEM((groups, 2 * cols, depth), F32),
+            pltpu.VMEM((panel, 2, slots), F32),
+            pltpu.VMEM((bands * groups, own, 2, slots), F32),
+            dma((2,)),
+            dma((groups,)),
+            dma((groups,)),
+            dma((groups,)),
+            dma((groups,)),
+            dma((bands * groups,)),
+            dma((bands * groups,)),
+            dma((3,)),
+        ],
+        compiler_params=pltpu.CompilerParams(
+            collective_id=0, has_side_effects=True, vmem_limit_bytes=48 * 1024 * 1024
+        ),
+    )(coefficients, rot, potential)
+
+
 def apply_kernel(
-    box, window, radix, chunk, val_ref, row_ref, col_ref, pot_ref, right_ref, left_ref, back_ref, twist_ref, out_ref, acc
+    box, window, radix, val_ref, row_ref, col_ref, pot_ref, right_ref, left_ref, back_ref, twist_ref, out_ref, acc
 ):
     coarse = window // radix
     rows = radix * window
     cols = coarse * window
     wide = radix * box
-    slots = val_ref.shape[1]
+    chunk = val_ref.shape[2]
     acc[...] = jnp.zeros_like(acc)
 
     def scatter(step, carry):
@@ -91,7 +221,7 @@
         picks = lax.broadcasted_iota(jnp.int32, (rows, chunk), 0) == row_id
         onehot = jnp.where(picks, 1.0, 0.0).astype(BF16)
         hits = lax.broadcasted_iota(jnp.int32, (cols, chunk), 0) == col_id
-        high, low = split_parts(val_ref[:, at])
+        high, low = split_parts(val_ref[step])
         high, low = high.astype(F32), low.astype(F32)
         placed = [
             jnp.where(hits, part[c : c + 1, :], 0.0).astype(BF16)
@@ -106,7 +236,7 @@
         )
         return carry
 
-    lax.fori_loop(0, slots // chunk, scatter, 0)
+    lax.fori_loop(0, val_ref.shape[0], scatter, 0)
     grid_field = acc[:, : 2 * cols] + acc[:, 2 * cols :]
 
     right = [block(right_ref[i, 0], right_ref[i, 1]) for i in range(2)]
@@ -124,8 +254,13 @@
     )
     left = [block(left_ref[i, 0], -left_ref[i, 1]) for i in range(2)]
     space = dot3(left, split_parts(turned))
+    per = pot_ref.shape[0] // (box // radix)
     pot = jnp.concatenate(
-        [pot_ref[:, k * wide : (k + 1) * wide] for k in range(box // radix)], axis=0
+        [
+            jnp.concatenate([pot_ref[k * per + i] for i in range(per)], axis=1)
+            for k in range(box // radix)
+        ],
+        axis=0,
     )
     space = space * jnp.concatenate([pot, pot], axis=0)
     back = [block(back_ref[i, 0], back_ref[i, 1]) for i in range(2)]
@@ -159,12 +294,10 @@
 
 
 def apply_band(values, row_id, col_id, pot_full, window, radix, consts):
-    box = pot_full.shape[0]
-    slots = values.shape[1]
-    chunk = math.gcd(slots, 1024)
+    box = pot_full.shape[1]
     vmem = pl.BlockSpec(memory_space=pltpu.VMEM)
     return pl.pallas_call(
-        functools.partial(apply_kernel, box, window, radix, chunk),
+        functools.partial(apply_kernel, box, window, radix),
         out_shape=jax.ShapeDtypeStruct((2, window, window * window), F32),
         in_specs=[vmem] * 8,
         out_specs=vmem,
@@ -174,12 +307,8 @@
 
 
 def per_device(coefficients, rotation, potential, index_map, counts):
-    mixer = lax.all_gather(mixing(rotation), "ga", axis=0, tiled=True)
-    pot_full = lax.all_gather(potential, "ga", axis=1, tiled=True)
-    band_local = coefficients.shape[0]
-    slot_local = coefficients.shape[2]
-    flat_coeffs = coefficients.reshape(2 * band_local, slot_local)
-    box = pot_full.shape[0]
+    values, pot_full = exchange(coefficients, rotation, potential)
+    box = pot_full.shape[1]
     window = box // 2
     half = window // 2
     radix = math.isqrt(box)
@@ -195,18 +324,10 @@
     col_id = (cell_y // radix * window + cell_z)[None]
     consts = [jnp.asarray(t) for t in tables(box, window, radix)]
 
-    product = jnp.dot(mixer, flat_coeffs, precision=lax.Precision.HIGH)
-    panel_rows = mixer.shape[0] // 2
-    summed = lax.psum_scatter(
-        product.reshape(panel_rows, 2, slot_local), "band", scatter_dimension=0, tiled=True
-    )
-    groups = lax.axis_size("ga")
-    grouped = summed.reshape(groups, summed.shape[0] // groups, 2, slot_local)
-    values = lax.all_to_all(grouped, "ga", split_axis=0, concat_axis=3, tiled=True)[0]
     return jnp.stack(
         [
-            apply_band(values[i], row_id, col_id, pot_full, window, radix, consts)
-            for i in range(values.shape[0])
+            apply_band(values[:, i], row_id, col_id, pot_full, window, radix, consts)
+            for i in range(values.shape[1])
         ]
     )
 

time: 139 us -> 66.4 us (0.48)
  Pallas kernels: 12.3 us -> 58.4 us
  blocking collectives: 45.3 us -> 0 us
  waiting for transfers between devices: 42.9 us -> 0 us
  between operations: 14.9 us -> 0.03 us
  starting transfers between devices: 6.79 us -> 0 us
  local copies, waits for them, and re-layouts: 10.6 us -> 5.37 us
  matrix products: 4.4 us -> 0 us
    pallas_call x1 -> x2, Pallas kernels: 12.3 us -> 58.4 us  [the longest x1 44.4 us: exchange(): pl.pallas_call(functools.partial(exchange_kernel, bands, groups), out_sha...]
    all_gather x1 -> x0, blocking collectives: 45.3 us -> none  [per_device(): mixer = lax.all_gather(mixing(rotation), 'ga', axis=0, tiled=True)]
    all_gather x1 -> x0, waiting for transfers between devices: 32.7 us -> none  [per_device(): pot_full = lax.all_gather(potential, 'ga', axis=1, tiled=True)]
    reshape x2 -> x1, local copies, waits for them, and re-layouts: 7.6 us -> 0.74 us  [exchange(): rot = rotation.transpose(0, 2, 1).reshape(1, 2 * cols, depth)]
    all_to_all x1 -> x0, waiting for transfers between devices: 6.77 us -> none  [per_device(): lax.all_to_all(grouped, 'ga', split_axis=0, concat_axis=3, tiled=True)[0]]
    all_to_all x1 -> x0, starting transfers between devices: 6.75 us -> none  [per_device(): lax.all_to_all(grouped, 'ga', split_axis=0, concat_axis=3, tiled=True)[0]]
    dot_general x1 -> x0, matrix products: 4.4 us -> none  [per_device(): product = jnp.dot(mixer, flat_coeffs, precision=lax.Precision.HIGH)]
    unnamed x8 -> x9, local copies, waits for them, and re-layouts: 1.26 us -> 4.63 us
  transfers between devices with their start and end apart: 3 -> 0, of which waited for: 3 -> 0; matrix products, arithmetic and copies ran while one was open for 2% -> 0% of each run, Pallas kernels for 0% -> 0%
where the time goes in v2:
time: 66.4 us; the launch traced here: 66 us
  Pallas kernels  58.4 us (88%)
  local copies, waits for them, and re-layouts  5.37 us (8%)
  other arithmetic  2.25 us (3%)
    pallas_call x1, Pallas kernels, exchange(): pl.pallas_call(functools.partial(exchange_kernel, bands, groups), out_sha...  44.4 us
    pallas_call x1, Pallas kernels, apply_band(): pl.pallas_call(functools.partial(apply_kernel, box, window, radix), out_s...  14 us
    unnamed x9, local copies, waits for them, and re-layouts  4.63 us
    add x1, other arithmetic, per_device(): col_id = (cell_y // radix * window + cell_z)[None]  1.52 us

profile of v2, /device:TPU:0, one launch (start us, length us, event | category | flops | bytes accessed | tf_op | source)
XLA Modules:
  0.0 66.0 jit_solution(12868656639762857262)
XLA Ops:
  0.0 0.7 %fusion.13 = pred[2,4,8,128]{3,2,1,0:T(8,128)(4,1)S(1)} fusion(s32[16]{0:T(128)} %param.13), kind=kLoop, calls=%fused_computation.41 | loop fusion | flops 8192 | bytes 8256
  0.7 0.7 %reshape.8.rot_ref = f32[1,4,1024]{2,1,0:T(4,128)S(1)} reshape(f32[2,2,1024]{2,1,0:T(2,128)} %bitcast.12) | data formatting | bytes 32768 | tf_op jit(solution)/shard_map/reshape | solution.py:175
  1.5 1.5 %fusion.12 = (s32[8192]{0:T(1024)}, s32[8192]{0:T(1024)}) fusion(s32[8192]{0:T(1024)} %param.12, pred[8192]{0:T(1024)(128)(4,1)S(1)} %bitcast.11), kind=kLoop, calls=%fused_computation.37 | loop fusion | flops 868352 | bytes 106496 | tf_op jit(solution)/shard_map/add | solution.py:324
  3.0 0.0 copy-start
  3.0 2.2 %copy-done = f32[1024,2,512]{2,1,0:T(2,128)S(1)} copy-done((f32[1024,2,512]{2,1,0:T(2,128)S(1)}, f32[1024,2,512]{2,1,0:T(2,128)}, u32[]{:S(2)}) %copy-start) | copy-done | bytes 4194328
  5.2 0.0 copy-start.2
  5.2 0.8 %copy-done.2 = f32[64,256]{1,0:T(8,128)S(1)} copy-done((f32[64,256]{1,0:T(8,128)S(1)}, f32[64,256]{1,0:T(8,128)}, u32[]{:S(2)}) %copy-start.2) | copy-done | bytes 65560
  6.0 44.4 %shard_map.91 = (f32[16,1,2,512]{3,2,1,0:T(2,128)S(1)}, f32[16,64,256]{2,1,0:T(8,128)S(1)}) custom-call(f32[1024,2,512]{2,1,0:T(2,128)S(1)} %copy-done, f32[1,4,1024]{2,1,0:T(4,128)S(1)} %reshape.8.rot_ref, f32[64,256]{1,0:T(8,128)S(1)} %copy-done.2), custom_call_target="tpu_custom_call" | custom-call | tf_op jit(solution)/shard_map/pallas_call | solution.py:179
  50.4 0.0 copy-start.1
  50.4 1.0 %copy-done.1 = f32[16,64,256]{2,1,0:T(8,128)} copy-done((f32[16,64,256]{2,1,0:T(8,128)}, f32[16,64,256]{2,1,0:T(8,128)S(1)}, u32[]{:S(2)}) %copy-start.1) | copy-done | bytes 1048600
  51.4 0.0 copy-start.3
  51.4 0.6 copy-done.3
  52.0 14.0 %shard_map.92 = f32[2,32,1024]{2,1,0:T(8,128)} custom-call(f32[16,2,512]{2,1,0:T(2,128)} %bitcast.8, s32[1,8192]{1,0:T(1,128)} %bitcast.10, s32[1,8192]{1,0:T(1,128)} %bitcast.9, f32[16,64,256]{2,1,0:T(8,128)} %copy-done.1, bf16[2,2,128,512]{3,2,1,0:T(8,128)(2,1)} %constant.92.clone.right_ref, bf16[2,2,512,256]{3,2,1,0:T(8,128)(2,1)} %constant.93.clone.left_ref, ...), custom_call_target="tpu_custom_call" | custom-call | tf_op jit(solution)/shard_map/pallas_call | solution.py:299
  (1 shorter events, 0.0 us)
Async XLA Ops:
  3.0 2.2 %copy-start = (f32[1024,2,512]{2,1,0:T(2,128)S(1)}, f32[1024,2,512]{2,1,0:T(2,128)}, u32[]{:S(2)}) copy-start(f32[1024,2,512]{2,1,0:T(2,128)} %coef_hbm.1) | copy-start | bytes 12582916
  5.2 0.8 %copy-start.2 = (f32[64,256]{1,0:T(8,128)S(1)}, f32[64,256]{1,0:T(8,128)}, u32[]{:S(2)}) copy-start(f32[64,256]{1,0:T(8,128)} %pot_hbm.1) | copy-start | bytes 196612
  50.4 1.0 %copy-start.1 = (f32[16,64,256]{2,1,0:T(8,128)}, f32[16,64,256]{2,1,0:T(8,128)S(1)}, u32[]{:S(2)}) copy-start(f32[16,64,256]{2,1,0:T(8,128)S(1)} %get-tuple-element.8.pot_ref) | copy-start | bytes 3145732
  51.4 0.6 copy-start.3

commit v3 on v2

--- a/solution.py
+++ b/solution.py
@@ -67,7 +67,7 @@
 
 def exchange_kernel(
     bands, groups, coef_hbm, rot_ref, pot_hbm, val_ref, pot_out, coef, rots, prod, land,
-    coef_sem, rot_send, rot_recv, pot_send, pot_recv, val_send, val_recv, self_sem
+    coef_sem, rot_send, rot_recv, pot_send, pot_recv, pass_send, pass_recv, val_send, val_recv, self_sem
 ):
     band = lax.axis_index("band")
     me = lax.axis_index("ga")
@@ -75,6 +75,8 @@
     flat = band * groups + me
     cols = rot_ref.shape[1] // 2
     own = land.shape[1]
+    rows = pot_hbm.shape[0] // bands
+    share = pl.ds(pl.multiple_of(band * rows, rows), rows)
 
     loads = [
         pltpu.make_async_copy(coef_hbm.at[:, c, :], coef.at[c], coef_sem.at[c]) for c in range(2)
@@ -108,9 +110,17 @@
 
     def pot_copy(to, slot):
         return pltpu.make_async_remote_copy(
-            src_ref=pot_hbm, dst_ref=pot_out.at[slot],
+            src_ref=pot_hbm.at[share], dst_ref=pot_out.at[slot, share],
             send_sem=pot_send.at[to], recv_sem=pot_recv.at[slot],
             device_id={"band": band, "ga": to}, device_id_type=pl.DeviceIdType.MESH,
+        )
+
+    def pass_copy(slot, to, holder):
+        held = pl.ds(pl.multiple_of(holder * rows, rows), rows)
+        return pltpu.make_async_remote_copy(
+            src_ref=pot_out.at[slot, held], dst_ref=pot_out.at[slot, held],
+            send_sem=pass_send.at[to, slot], recv_sem=pass_recv.at[holder, slot],
+            device_id={"band": to, "ga": me}, device_id_type=pl.DeviceIdType.MESH,
         )
 
     def val_copy(to, slot):
@@ -153,6 +163,12 @@
     val_self = pltpu.make_async_copy(prod.at[pl.ds(flat * own, own)], land.at[flat], self_sem.at[2])
     val_self.start()
     each(total, flat, lambda to: val_copy(to, flat).start())
+
+    def relay(src):
+        pot_copy(src, src).wait_recv()
+        each(bands, band, lambda to: pass_copy(src, to, band).start())
+
+    each(groups, me, relay)
     val_self.wait()
     each(total, flat, lambda src: val_copy(src, src).wait_recv())
     summed = land[0:groups]
@@ -162,8 +178,9 @@
     each(total, flat, lambda to: val_copy(to, flat).wait_send())
     each(groups, me, lambda to: rot_copy(to, me).wait_send())
     pot_self.wait()
-    each(groups, me, lambda src: pot_copy(src, src).wait_recv())
     each(groups, me, lambda to: pot_copy(to, me).wait_send())
+    each(groups, me, lambda src: each(bands, band, lambda b: pass_copy(src, b, b).wait_recv()))
+    each(groups, me, lambda src: each(bands, band, lambda b: pass_copy(src, b, band).wait_send()))
 
 
 def exchange(coefficients, rotation, potential):
@@ -194,6 +211,8 @@
             dma((groups,)),
             dma((groups,)),
             dma((groups,)),
+            dma((bands, groups)),
+            dma((bands, groups)),
             dma((bands * groups,)),
             dma((bands * groups,)),
             dma((3,)),

time: 66.4 us -> 55.8 us (0.84)
  Pallas kernels: 58.4 us -> 47.9 us
    pallas_call x1, Pallas kernels: 44.4 us -> 33.8 us  [exchange(): pl.pallas_call(functools.partial(exchange_kernel, bands, groups), out_sha...]
where the time goes in v3:
time: 55.8 us; the launch traced here: 55.5 us
  Pallas kernels  47.9 us (86%)
  local copies, waits for them, and re-layouts  5.37 us (10%)
  other arithmetic  2.25 us (4%)
    pallas_call x1, Pallas kernels, exchange(): pl.pallas_call(functools.partial(exchange_kernel, bands, groups), out_sha...  33.8 us
    pallas_call x1, Pallas kernels, apply_band(): pl.pallas_call(functools.partial(apply_kernel, box, window, radix), out_s...  14 us
    unnamed x9, local copies, waits for them, and re-layouts  4.63 us
    add x1, other arithmetic, per_device(): col_id = (cell_y // radix * window + cell_z)[None]  1.52 us

profile of v3, /device:TPU:0, one launch (start us, length us, event | category | flops | bytes accessed | tf_op | source)
XLA Modules:
  0.0 55.5 jit_solution(16490340461762564929)
XLA Ops:
  0.0 0.7 %fusion.13 = pred[2,4,8,128]{3,2,1,0:T(8,128)(4,1)S(1)} fusion(s32[16]{0:T(128)} %param.13), kind=kLoop, calls=%fused_computation.41 | loop fusion | flops 8192 | bytes 8256
  0.7 0.7 %reshape.8.rot_ref = f32[1,4,1024]{2,1,0:T(4,128)S(1)} reshape(f32[2,2,1024]{2,1,0:T(2,128)} %bitcast.12) | data formatting | bytes 32768 | tf_op jit(solution)/shard_map/reshape | solution.py:192
  1.5 1.5 %fusion.12 = (s32[8192]{0:T(1024)}, s32[8192]{0:T(1024)}) fusion(s32[8192]{0:T(1024)} %param.12, pred[8192]{0:T(1024)(128)(4,1)S(1)} %bitcast.11), kind=kLoop, calls=%fused_computation.37 | loop fusion | flops 868352 | bytes 106496 | tf_op jit(solution)/shard_map/add | solution.py:343
  3.0 0.0 copy-start
  3.0 2.2 %copy-done = f32[1024,2,512]{2,1,0:T(2,128)S(1)} copy-done((f32[1024,2,512]{2,1,0:T(2,128)S(1)}, f32[1024,2,512]{2,1,0:T(2,128)}, u32[]{:S(2)}) %copy-start) | copy-done | bytes 4194328
  5.2 0.0 copy-start.2
  5.2 0.8 %copy-done.2 = f32[64,256]{1,0:T(8,128)S(1)} copy-done((f32[64,256]{1,0:T(8,128)S(1)}, f32[64,256]{1,0:T(8,128)}, u32[]{:S(2)}) %copy-start.2) | copy-done | bytes 65560
  6.0 33.8 %shard_map.91 = (f32[16,1,2,512]{3,2,1,0:T(2,128)S(1)}, f32[16,64,256]{2,1,0:T(8,128)S(1)}) custom-call(f32[1024,2,512]{2,1,0:T(2,128)S(1)} %copy-done, f32[1,4,1024]{2,1,0:T(4,128)S(1)} %reshape.8.rot_ref, f32[64,256]{1,0:T(8,128)S(1)} %copy-done.2), custom_call_target="tpu_custom_call" | custom-call | tf_op jit(solution)/shard_map/pallas_call | solution.py:196
  39.9 0.0 copy-start.1
  39.9 1.0 %copy-done.1 = f32[16,64,256]{2,1,0:T(8,128)} copy-done((f32[16,64,256]{2,1,0:T(8,128)}, f32[16,64,256]{2,1,0:T(8,128)S(1)}, u32[]{:S(2)}) %copy-start.1) | copy-done | bytes 1048600
  40.8 0.0 copy-start.3
  40.8 0.6 %copy-done.3 = f32[16,1,2,512]{3,2,1,0:T(2,128)} copy-done((f32[16,1,2,512]{3,2,1,0:T(2,128)}, f32[16,1,2,512]{3,2,1,0:T(2,128)S(1)}, u32[]{:S(2)}) %copy-start.3) | copy-done | bytes 65560
  41.5 14.0 %shard_map.92 = f32[2,32,1024]{2,1,0:T(8,128)} custom-call(f32[16,2,512]{2,1,0:T(2,128)} %bitcast.8, s32[1,8192]{1,0:T(1,128)} %bitcast.10, s32[1,8192]{1,0:T(1,128)} %bitcast.9, f32[16,64,256]{2,1,0:T(8,128)} %copy-done.1, bf16[2,2,128,512]{3,2,1,0:T(8,128)(2,1)} %constant.92.clone.right_ref, bf16[2,2,512,256]{3,2,1,0:T(8,128)(2,1)} %constant.93.clone.left_ref, ...), custom_call_target="tpu_custom_call" | custom-call | tf_op jit(solution)/shard_map/pallas_call | solution.py:318
  (1 shorter events, 0.0 us)
Async XLA Ops:
  3.0 2.2 %copy-start = (f32[1024,2,512]{2,1,0:T(2,128)S(1)}, f32[1024,2,512]{2,1,0:T(2,128)}, u32[]{:S(2)}) copy-start(f32[1024,2,512]{2,1,0:T(2,128)} %coef_hbm.1) | copy-start | bytes 12582916
  5.2 0.8 %copy-start.2 = (f32[64,256]{1,0:T(8,128)S(1)}, f32[64,256]{1,0:T(8,128)}, u32[]{:S(2)}) copy-start(f32[64,256]{1,0:T(8,128)} %pot_hbm.1) | copy-start | bytes 196612
  39.9 1.0 %copy-start.1 = (f32[16,64,256]{2,1,0:T(8,128)}, f32[16,64,256]{2,1,0:T(8,128)S(1)}, u32[]{:S(2)}) copy-start(f32[16,64,256]{2,1,0:T(8,128)S(1)} %get-tuple-element.8.pot_ref) | copy-start | bytes 3145732
  40.8 0.6 %copy-start.3 = (f32[16,1,2,512]{3,2,1,0:T(2,128)}, f32[16,1,2,512]{3,2,1,0:T(2,128)S(1)}, u32[]{:S(2)}) copy-start(f32[16,1,2,512]{3,2,1,0:T(2,128)S(1)} %get-tuple-element.7) | copy-start | bytes 196612

commit v4 on v3

--- a/solution.py
+++ b/solution.py
@@ -65,8 +65,9 @@
     return jnp.concatenate([upper, lower], axis=0)
 
 
-def exchange_kernel(
-    bands, groups, coef_hbm, rot_ref, pot_hbm, val_ref, pot_out, coef, rots, prod, land,
+def whole_kernel(
+    bands, groups, box, window, radix, coef_hbm, rot_ref, pot_hbm, row_ref, col_ref,
+    right_ref, left_ref, back_ref, twist_ref, out_ref, pot_out, acc, coef, rots, prod, land, vals,
     coef_sem, rot_send, rot_recv, pot_send, pot_recv, pass_send, pass_recv, val_send, val_recv, self_sem
 ):
     band = lax.axis_index("band")
@@ -174,16 +175,24 @@
     summed = land[0:groups]
     for b in range(1, bands):
         summed = summed + land[b * groups : (b + 1) * groups]
-    val_ref[...] = summed
+    vals[...] = summed
+
+    def pot_ready():
+        pot_self.wait()
+        each(groups, me, lambda src: each(bands, band, lambda b: pass_copy(src, b, b).wait_recv()))
+
+    for i in range(own):
+        apply_kernel(
+            box, window, radix, i, pot_ready if i == 0 else None, vals, row_ref, col_ref, pot_out,
+            right_ref, left_ref, back_ref, twist_ref, out_ref, acc
+        )
     each(total, flat, lambda to: val_copy(to, flat).wait_send())
     each(groups, me, lambda to: rot_copy(to, me).wait_send())
-    pot_self.wait()
     each(groups, me, lambda to: pot_copy(to, me).wait_send())
-    each(groups, me, lambda src: each(bands, band, lambda b: pass_copy(src, b, b).wait_recv()))
     each(groups, me, lambda src: each(bands, band, lambda b: pass_copy(src, b, band).wait_send()))
 
 
-def exchange(coefficients, rotation, potential):
+def run(coefficients, rotation, potential, row_id, col_id, consts, box, window, radix):
     bands, groups = lax.axis_size("band"), lax.axis_size("ga")
     depth, _, slots = coefficients.shape
     cols = rotation.shape[2]
@@ -194,18 +203,18 @@
     vmem = pl.BlockSpec(memory_space=pltpu.VMEM)
     dma = pltpu.SemaphoreType.DMA
     return pl.pallas_call(
-        functools.partial(exchange_kernel, bands, groups),
-        out_shape=(
-            jax.ShapeDtypeStruct((groups, own, 2, slots), F32),
-            jax.ShapeDtypeStruct((groups,) + potential.shape, F32),
-        ),
-        in_specs=[hbm, vmem, hbm],
-        out_specs=(vmem, hbm),
+        functools.partial(whole_kernel, bands, groups, box, window, radix),
+        out_shape=jax.ShapeDtypeStruct((own, 2, window, window * window), F32),
+        in_specs=[hbm, vmem, hbm] + [vmem] * 6,
+        out_specs=vmem,
         scratch_shapes=[
+            pltpu.VMEM((groups,) + potential.shape, F32),
+            pltpu.VMEM((radix * window, 4 * (window // radix) * window), F32),
             pltpu.VMEM((2, depth, slots), F32),
             pltpu.VMEM((groups, 2 * cols, depth), F32),
             pltpu.VMEM((panel, 2, slots), F32),
             pltpu.VMEM((bands * groups, own, 2, slots), F32),
+            pltpu.VMEM((groups, own, 2, slots), F32),
             dma((2,)),
             dma((groups,)),
             dma((groups,)),
@@ -218,19 +227,19 @@
             dma((3,)),
         ],
         compiler_params=pltpu.CompilerParams(
-            collective_id=0, has_side_effects=True, vmem_limit_bytes=48 * 1024 * 1024
+            collective_id=0, has_side_effects=True, vmem_limit_bytes=60 * 1024 * 1024
         ),
-    )(coefficients, rot, potential)
+    )(coefficients, rot, potential, row_id, col_id, *consts)
 
 
 def apply_kernel(
-    box, window, radix, val_ref, row_ref, col_ref, pot_ref, right_ref, left_ref, back_ref, twist_ref, out_ref, acc
+    box, window, radix, index, pot_ready, val_ref, row_ref, col_ref, pot_ref, right_ref, left_ref, back_ref, twist_ref, out_ref, acc
 ):
     coarse = window // radix
     rows = radix * window
     cols = coarse * window
     wide = radix * box
-    chunk = val_ref.shape[2]
+    chunk = val_ref.shape[3]
     acc[...] = jnp.zeros_like(acc)
 
     def scatter(step, carry):
@@ -240,7 +249,7 @@
         picks = lax.broadcasted_iota(jnp.int32, (rows, chunk), 0) == row_id
         onehot = jnp.where(picks, 1.0, 0.0).astype(BF16)
         hits = lax.broadcasted_iota(jnp.int32, (cols, chunk), 0) == col_id
-        high, low = split_parts(val_ref[step])
+        high, low = split_parts(val_ref[step, index])
         high, low = high.astype(F32), low.astype(F32)
         placed = [
             jnp.where(hits, part[c : c + 1, :], 0.0).astype(BF16)
@@ -273,6 +282,8 @@
     )
     left = [block(left_ref[i, 0], -left_ref[i, 1]) for i in range(2)]
     space = dot3(left, split_parts(turned))
+    if pot_ready is not None:
+        pot_ready()
     per = pot_ref.shape[0] // (box // radix)
     pot = jnp.concatenate(
         [
@@ -309,25 +320,11 @@
             for hi in range(coarse)
             for lo in range(radix)
         ]
-        out_ref[c] = jnp.concatenate(pieces, axis=1)
-
-
-def apply_band(values, row_id, col_id, pot_full, window, radix, consts):
-    box = pot_full.shape[1]
-    vmem = pl.BlockSpec(memory_space=pltpu.VMEM)
-    return pl.pallas_call(
-        functools.partial(apply_kernel, box, window, radix),
-        out_shape=jax.ShapeDtypeStruct((2, window, window * window), F32),
-        in_specs=[vmem] * 8,
-        out_specs=vmem,
-        scratch_shapes=[pltpu.VMEM((radix * window, 4 * (window // radix) * window), F32)],
-        compiler_params=pltpu.CompilerParams(vmem_limit_bytes=60 * 1024 * 1024),
-    )(values, row_id, col_id, pot_full, *consts)
+        out_ref[index, c] = jnp.concatenate(pieces, axis=1)
 
 
 def per_device(coefficients, rotation, potential, index_map, counts):
-    values, pot_full = exchange(coefficients, rotation, potential)
-    box = pot_full.shape[1]
+    box = potential.shape[0]
     window = box // 2
     half = window // 2
     radix = math.isqrt(box)
@@ -343,12 +340,7 @@
     col_id = (cell_y // radix * window + cell_z)[None]
     consts = [jnp.asarray(t) for t in tables(box, window, radix)]
 
-    return jnp.stack(
-        [
-            apply_band(values[:, i], row_id, col_id, pot_full, window, radix, consts)
-            for i in range(values.shape[1])
-        ]
-    )
+    return run(coefficients, rotation, potential, row_id, col_id, consts, box, window, radix)
 
 
 def solution(mesh):

time: 55.8 us -> 50.3 us (0.901)
  Pallas kernels: 47.9 us -> 44.8 us
  local copies, waits for them, and re-layouts: 5.37 us -> 3.03 us
    pallas_call x2 -> x1, Pallas kernels: 47.9 us -> 44.8 us  [run(): pl.pallas_call(functools.partial(whole_kernel, bands, groups, box, window...]
    unnamed x9 -> x2, local copies, waits for them, and re-layouts: 4.63 us -> 1.69 us
    reshape x1, local copies, waits for them, and re-layouts: 0.74 us -> 1.34 us  [run(): rot = rotation.transpose(0, 2, 1).reshape(1, 2 * cols, depth)]
where the time goes in v4:
time: 50.3 us; the launch traced here: 50 us
  Pallas kernels  44.8 us (89%)
  local copies, waits for them, and re-layouts  3.03 us (6%)
  other arithmetic  2.24 us (4%)
    pallas_call x1, Pallas kernels, run(): pl.pallas_call(functools.partial(whole_kernel, bands, groups, box, window...  44.8 us
    unnamed x2, local copies, waits for them, and re-layouts  1.69 us
    add x1, other arithmetic, per_device(): col_id = (cell_y // radix * window + cell_z)[None]  1.52 us
    reshape x1, local copies, waits for them, and re-layouts, run(): rot = rotation.transpose(0, 2, 1).reshape(1, 2 * cols, depth)  1.34 us

profile of v4, /device:TPU:0, one launch (start us, length us, event | category | flops | bytes accessed | tf_op | source)
XLA Modules:
  0.0 50.0 jit_solution(18214845360536928192)
XLA Ops:
  0.0 0.7 %fusion.13 = pred[2,4,8,128]{3,2,1,0:T(8,128)(4,1)S(1)} fusion(s32[16]{0:T(128)} %param.13), kind=kLoop, calls=%fused_computation.41 | loop fusion | flops 8192 | bytes 8256
  0.7 1.3 %reshape.8.rot_ref = f32[1,4,1024]{2,1,0:T(4,128)} reshape(f32[2,2,1024]{2,1,0:T(2,128)} %bitcast.9) | data formatting | bytes 32768 | tf_op jit(solution)/shard_map/reshape | solution.py:201
  2.1 1.5 %fusion.12 = (s32[8192]{0:T(1024)}, s32[8192]{0:T(1024)}) fusion(s32[8192]{0:T(1024)} %param.12, pred[8192]{0:T(1024)(128)(4,1)S(1)} %bitcast.8), kind=kLoop, calls=%fused_computation.37 | loop fusion | flops 868352 | bytes 106496 | tf_op jit(solution)/shard_map/add | solution.py:340
  3.6 44.8 %shard_map.91 = f32[1,2,32,1024]{3,2,1,0:T(8,128)} custom-call(f32[1024,2,512]{2,1,0:T(2,128)} %coef_hbm.1, f32[1,4,1024]{2,1,0:T(4,128)} %reshape.8.rot_ref, f32[64,256]{1,0:T(8,128)} %pot_hbm.1, s32[1,8192]{1,0:T(1,128)} %bitcast.7, s32[1,8192]{1,0:T(1,128)} %bitcast.6, bf16[2,2,128,512]{3,2,1,0:T(8,128)(2,1)} %constant.92.clone.right_ref, ...), custom_call_target="tpu_custom_call" | custom-call | tf_op jit(solution)/shard_map/pallas_call | solution.py:205
  48.4 1.7 %copy.12 = f32[1,2,32,1024]{3,2,1,0:T(8,128)} copy(f32[1,2,32,1024]{3,2,1,0:T(8,128)} %shard_map.91) | data formatting | bytes 524288
  (1 shorter events, 0.0 us)

commit v5 on v4

--- a/solution.py
+++ b/solution.py
@@ -67,7 +67,7 @@
 
 def whole_kernel(
     bands, groups, box, window, radix, coef_hbm, rot_ref, pot_hbm, row_ref, col_ref,
-    right_ref, left_ref, back_ref, twist_ref, out_ref, pot_out, acc, coef, rots, prod, land, vals,
+    right_hbm, left_hbm, back_hbm, twist_ref, out_ref, right_ref, left_ref, back_ref, tab_sem, pot_out, acc, coef, rots, prod, land, vals,
     coef_sem, rot_send, rot_recv, pot_send, pot_recv, pass_send, pass_recv, val_send, val_recv, self_sem
 ):
     band = lax.axis_index("band")
@@ -84,6 +84,14 @@
     ]
     for load in loads:
         load.start()
+    tabs = [
+        pltpu.make_async_copy(src, dst, tab_sem.at[i])
+        for i, (src, dst) in enumerate(
+            ((right_hbm, right_ref), (left_hbm, left_ref), (back_hbm, back_ref))
+        )
+    ]
+    for tab in tabs:
+        tab.start()
     rot_self = pltpu.make_async_copy(rot_ref.at[0], rots.at[me], self_sem.at[0])
     rot_self.start()
     pot_self = pltpu.make_async_copy(pot_hbm, pot_out.at[me], self_sem.at[1])
@@ -176,6 +184,8 @@
     for b in range(1, bands):
         summed = summed + land[b * groups : (b + 1) * groups]
     vals[...] = summed
+    for tab in tabs:
+        tab.wait()
 
     def pot_ready():
         pot_self.wait()
@@ -205,9 +215,11 @@
     return pl.pallas_call(
         functools.partial(whole_kernel, bands, groups, box, window, radix),
         out_shape=jax.ShapeDtypeStruct((own, 2, window, window * window), F32),
-        in_specs=[hbm, vmem, hbm] + [vmem] * 6,
+        in_specs=[hbm, vmem, hbm] + [vmem] * 2 + [hbm] * 3 + [vmem],
         out_specs=vmem,
         scratch_shapes=[
+            *[pltpu.VMEM(table.shape, table.dtype) for table in consts[:3]],
+            dma((3,)),
             pltpu.VMEM((groups,) + potential.shape, F32),
             pltpu.VMEM((radix * window, 4 * (window // radix) * window), F32),
             pltpu.VMEM((2, depth, slots), F32),

time: 50.3 us -> 49.4 us (0.982)
  Pallas kernels: 44.8 us -> 43.8 us
    pallas_call x1, Pallas kernels: 44.8 us -> 43.8 us  [run(): pl.pallas_call(functools.partial(whole_kernel, bands, groups, box, window...]
where the time goes in v5:
time: 49.4 us; the launch traced here: 49.1 us
  Pallas kernels  43.8 us (89%)
  local copies, waits for them, and re-layouts  3.03 us (6%)
  other arithmetic  2.24 us (5%)
    pallas_call x1, Pallas kernels, run(): pl.pallas_call(functools.partial(whole_kernel, bands, groups, box, window...  43.8 us
    unnamed x2, local copies, waits for them, and re-layouts  1.69 us
    add x1, other arithmetic, per_device(): col_id = (cell_y // radix * window + cell_z)[None]  1.52 us
    reshape x1, local copies, waits for them, and re-layouts, run(): rot = rotation.transpose(0, 2, 1).reshape(1, 2 * cols, depth)  1.34 us

profile of v5, /device:TPU:0, one launch (start us, length us, event | category | flops | bytes accessed | tf_op | source)
XLA Modules:
  0.0 49.1 jit_solution(9815922233460753711)
XLA Ops:
  0.0 0.7 %fusion.13 = pred[2,4,8,128]{3,2,1,0:T(8,128)(4,1)S(1)} fusion(s32[16]{0:T(128)} %param.13), kind=kLoop, calls=%fused_computation.41 | loop fusion | flops 8192 | bytes 8256
  0.7 1.3 %reshape.8.rot_ref = f32[1,4,1024]{2,1,0:T(4,128)} reshape(f32[2,2,1024]{2,1,0:T(2,128)} %bitcast.9) | data formatting | bytes 32768 | tf_op jit(solution)/shard_map/reshape | solution.py:211
  2.1 1.5 %fusion.12 = (s32[8192]{0:T(1024)}, s32[8192]{0:T(1024)}) fusion(s32[8192]{0:T(1024)} %param.12, pred[8192]{0:T(1024)(128)(4,1)S(1)} %bitcast.8), kind=kLoop, calls=%fused_computation.37 | loop fusion | flops 868352 | bytes 106496 | tf_op jit(solution)/shard_map/add | solution.py:352
  3.6 43.8 %shard_map.91 = f32[1,2,32,1024]{3,2,1,0:T(8,128)} custom-call(f32[1024,2,512]{2,1,0:T(2,128)} %coef_hbm.1, f32[1,4,1024]{2,1,0:T(4,128)} %reshape.8.rot_ref, f32[64,256]{1,0:T(8,128)} %pot_hbm.1, s32[1,8192]{1,0:T(1,128)} %bitcast.7, s32[1,8192]{1,0:T(1,128)} %bitcast.6, bf16[2,2,128,512]{3,2,1,0:T(8,128)(2,1)} %constant.92.clone.right_hbm, ...), custom_call_target="tpu_custom_call" | custom-call | tf_op jit(solution)/shard_map/pallas_call | solution.py:215
  47.4 1.7 %copy.12 = f32[1,2,32,1024]{3,2,1,0:T(8,128)} copy(f32[1,2,32,1024]{3,2,1,0:T(8,128)} %shard_map.91) | data formatting | bytes 524288
  (1 shorter events, 0.0 us)
